TPU v7x, 128 devices: a whole 4x4x4 slice. The times are simulated.
128 devices in a mesh: row: 32 (over x, y, core), col: 4 (over z).
Axes of the slice: x: 4, y: 4, z: 4, core: 2. Of those that a mesh axis runs over, the one named last changes fastest.
Arguments:
- right_side: bfloat16 [65536, 4096], P(('row', 'col')), may hold values from -6 to 6
- factor: bfloat16 [65536, 2048], P(('row', 'col')), may hold values from -0.125 to 0.125
- diag_inverse: bfloat16 [2048, 512], P('col'), as said below
- tile_mask: int32 [128, 4], P(('row', 'col')), may hold values from 0 to 1, as said below
- window_rows: int32 [4], replicated, may hold values from 0 to 127, as said below
Outputs:
- solution: bfloat16 [2048, 4096], P('row', 'col')
- updated_rhs: bfloat16 [65536, 4096], P(('row', 'col'))
Inputs may be any that keep to these rules, and one draw needn't show every extreme that they name: `window_rows`: distinct stored panel numbers, panels 0 and 127 always among them; panel p is stored on device p // 1 of row+col, and the window panels lie on different devices. `tile_mask`: 0 or 1; in the row of window panel k the entries of columns k and beyond are 0. `diag_inverse`: each tile is lower triangular.
All inputs are finite; a program needn't handle non-finite values.
Results may differ from a plain program's by a relative error of at most 0.0056.
Values may be sent and summed in bfloat16 or wider, within the bound.
A program may use at most 128 MiB of HBM per device.

v0:
```python
import jax
import jax.numpy as jnp
from jax import lax
from jax.sharding import PartitionSpec as P

AXES = ("row", "col")
NT = (((1,), (1,)), ((), ()))


def dot_nt(a, b):
    return lax.dot_general(a, b, NT, preferred_element_type=jnp.float32)


def body(right_side, factor, diag_inverse, tile_mask, window_rows):
    panel = diag_inverse.shape[1]
    window = factor.shape[1] // panel
    columns = right_side.shape[1]
    ncol = lax.axis_size("col")
    nrow = lax.axis_size("row")
    ndev = nrow * ncol
    width = columns // ndev
    col_index = lax.axis_index("col")
    row_index = lax.axis_index("row")
    me = row_index * ncol + col_index
    present = jnp.repeat(tile_mask[0] > 0, panel)
    masked = jnp.where(present[None, :], factor, jnp.zeros_like(factor))
    pieces = lax.all_to_all(
        right_side.T.reshape(ndev, width, panel), AXES, split_axis=0, concat_axis=0, tiled=True
    )
    lower = []
    for k in range(1, window):
        mine = me == window_rows[k]
        for j in range(k):
            tile = masked[:, j * panel : (j + 1) * panel]
            lower.append(jnp.where(mine, tile, jnp.zeros_like(tile)))
    lower = lax.psum(jnp.stack(lower), AXES)
    inverses = lax.all_gather(diag_inverse, "col", axis=0, tiled=True).reshape(window, panel, panel)
    solved = []
    for k in range(window):
        residual = lax.dynamic_index_in_dim(pieces, window_rows[k], 0, keepdims=False).astype(
            jnp.float32
        )
        for j in range(k):
            residual = residual - dot_nt(solved[j], lower[k * (k - 1) // 2 + j])
        solved.append(dot_nt(residual.astype(jnp.bfloat16), inverses[k]).astype(jnp.bfloat16))
    whole = lax.all_gather(jnp.concatenate(solved, axis=1), AXES, axis=0, tiled=True)
    updated = (right_side.astype(jnp.float32) - dot_nt(masked, whole)).astype(jnp.bfloat16)
    block_rows = window * panel // nrow
    block_cols = columns // ncol
    solution = lax.dynamic_slice(
        whole, (col_index * block_cols, row_index * block_rows), (block_cols, block_rows)
    ).T
    return (solution, updated)


def solution(mesh):
    in_specs = (P(AXES, None), P(AXES, None), P("col", None), P(AXES, None), P())
    out_specs = (P("row", "col"), P(AXES, None))
    return jax.shard_map(body, mesh=mesh, in_specs=in_specs, out_specs=out_specs, check_vma=False)
```

profile of v0, /device:TPU:1, one launch (start us, length us, event | category | flops | bytes accessed | tf_op | source)
XLA Modules:
  0.0 338.8 jit_solution(7828299529200578639)
XLA Ops:
  8.0 0.0 all-gather.3.cloned.1.call-start
  8.0 0.7 all-gather.3.cloned.1.call-update
  8.7 6.4 %copy.8 = bf16[512,4096]{0,1:T(8,128)(2,1)} copy(bf16[512,4096]{1,0:T(8,128)(2,1)} %param.5) | data formatting | bytes 8388608 | tf_op args[0]
  15.1 12.0 %all-to-all-start = ((bf16[128,32,512]{2,1,0:T(8,128)(2,1)}), bf16[128,32,512]{2,1,0:T(8,128)(2,1)}, u32[]{:S(2)}, u32[]{:S(2)}) async-start(bf16[128,32,512]{2,1,0:T(8,128)(2,1)} %bitcast.72), calls=%async_computation | async-start | bytes 8388608 | tf_op jit(solution)/shard_map/all_to_all | solution.py:27
  27.1 0.0 all-reduce.2.cloned.1.call-start
  27.2 0.1 broadcast_bitcast_fusion
  27.3 0.6 fusion.16
  29.8 1.8 broadcast_select_fusion
  31.5 0.9 bitcast_dynamic-update-slice_fusion.4
  32.5 1.0 bitcast_dynamic-update-slice_fusion.3
  33.4 0.9 bitcast_dynamic-update-slice_fusion.2
  34.3 0.9 bitcast_dynamic-update-slice_fusion.1
  35.3 0.9 bitcast_dynamic-update-slice_fusion
  36.2 0.9 fusion.7
  37.1 0.0 all-reduce.2.cloned.1.call-update
  37.1 0.0 all-gather.5.cloned.1.call-start
  44.7 46.7 %all-gather.3.cloned.1.call-done = bf16[2048,512]{1,0:T(8,128)(2,1)} async-done(((bf16[512,512]{1,0:T(8,128)(2,1)}), bf16[2048,512]{1,0:T(8,128)(2,1)}) %all-gather.3.cloned.1.call-update) | async-done | bytes 2097168 | tf_op jit(solution)/shard_map/all_gather | solution.py:37
  91.4 0.0 all-to-all-done
  91.4 1.3 convolution_convert_fusion.3
  92.7 133.6 %all-reduce.2.cloned.1.call-done = bf16[6,512,512]{2,1,0:T(8,128)(2,1)} async-done(((bf16[6,512,512]{2,1,0:T(8,128)(2,1)}), bf16[6,512,512]{2,1,0:T(8,128)(2,1)}) %all-reduce.2.cloned.1.call-update) | async-done | bytes 3145744 | tf_op jit(solution)/shard_map/psum | solution.py:36
  226.3 1.3 convolution_subtract_fusion.4
  227.6 1.6 convolution_convert_fusion.2
  229.3 1.3 convolution_subtract_fusion.2
  230.6 1.6 convolution_convert_fusion.1
  232.2 1.3 convolution_subtract_fusion.1
  233.6 1.6 convolution_convert_fusion
  235.2 0.7 pad_maximum_fusion
  235.9 0.0 all-gather.5.cloned.1.call-update
  235.9 79.1 %all-gather.5.cloned.1.call-done = bf16[4096,2048]{1,0:T(8,128)(2,1)} async-done(((bf16[32,2048]{1,0:T(8,128)(2,1)}), bf16[4096,2048]{1,0:T(8,128)(2,1)}) %all-gather.5.cloned.1.call-update) | async-done | bytes 16777232 | tf_op jit(solution)/shard_map/all_gather | solution.py:46
  315.1 1.1 dynamic-slice_bitcast_fusion
  316.2 0.8 copy.9
  317.0 14.4 %subtract_convert_fusion = bf16[512,4096]{1,0:T(8,128)(2,1)} fusion(bf16[512,4096]{1,0:T(8,128)(2,1)} %param.5, bf16[512,2048]{1,0:T(8,128)(2,1)S(1)} %broadcast_select_fusion, bf16[4096,2048]{1,0:T(8,128)(2,1)} %all-gather.5.cloned.1.call-done), kind=kOutput, calls=%fused_computation | convolution fusion | flops 8596226048 | bytes 27262976 | tf_op jit(solution)/shard_map/dot_general | solution.py:11
  (6 shorter events, 0.0 us)
Async XLA Ops:
  8.0 83.4 %all-gather.3.cloned.1.call-start = ((), (), s32[]{:S(2)}) async-start(), calls=%async_computation.1 | async-start | bytes 2621440 | tf_op jit(solution)/shard_map/all_gather | solution.py:37
  15.1 12.0 %copy-start.1 = (s32[1,4]{1,0:T(1,128)S(1)}, s32[1,4]{1,0:T(1,128)}, u32[]{:S(2)}) copy-start(s32[1,4]{1,0:T(1,128)} %param.8) | copy-start | bytes 52
  15.1 12.1 %copy-start = (s32[4]{0:T(128)S(1)}, s32[4]{0:T(128)}, u32[]{:S(2)}) copy-start(s32[4]{0:T(128)} %param.9) | copy-start | bytes 52
  15.1 76.2 %all-to-all-start = ((bf16[128,32,512]{2,1,0:T(8,128)(2,1)}), bf16[128,32,512]{2,1,0:T(8,128)(2,1)}, u32[]{:S(2)}, u32[]{:S(2)}) async-start(bf16[128,32,512]{2,1,0:T(8,128)(2,1)} %bitcast.72), calls=%async_computation | async-start | bytes 8388608 | tf_op jit(solution)/shard_map/all_to_all | solution.py:27
  27.1 199.2 %all-reduce.2.cloned.1.call-start = ((), (), s32[]{:S(2)}) async-start(), calls=%async_computation.2 | async-start | bytes 6291456 | tf_op jit(solution)/shard_map/psum | solution.py:36
  37.1 278.0 %all-gather.5.cloned.1.call-start = ((), (), s32[]{:S(2)}) async-start(), calls=%async_computation.3 | async-start | bytes 16908288 | tf_op jit(solution)/shard_map/all_gather | solution.py:46
Sparse Core Ops, SparseCore 0:
  10.6 80.7 all-gather.2
Sparse Core Ops, SparseCore 1:
  37.2 189.1 all-reduce.1
  236.0 79.0 all-gather.4
where the time goes:
time: 339 us
  waiting for transfers between devices  260 us (77%)
  between operations  25 us (7%)
  matrix products  24.5 us (7%)
  starting transfers between devices  12.1 us (4%)
  local copies, waits for them, and re-layouts  9 us (3%)
  other arithmetic  8.01 us (2%)
    psum x1, waiting for transfers between devices, body(): lower = lax.psum(jnp.stack(lower), AXES)  134 us
    all_gather x1, waiting for transfers between devices, body(): lax.all_gather(jnp.concatenate(solved, axis=1), AXES, axis=0, tiled=True)  79.1 us
    all_gather x1, waiting for transfers between devices, body(): lax.all_gather(diag_inverse, 'col', axis=0, tiled=True)  46.7 us
    dot_general x8, matrix products, dot_nt(): return lax.dot_general(a, b, NT, preferred_element_type=jnp.float32)  24.5 us
    all_to_all x1, starting transfers between devices, body(): lax.all_to_all(right_side.T.reshape(ndev, width, panel), AXES, split_axis...  12 us
    unnamed x8, local copies, waits for them, and re-layouts  7.29 us
  transfers between devices with their start and end apart: 4, of which 3 were waited for; matrix products, arithmetic and copies ran while one was open for 5% of the time, Pallas kernels for 0%

commit v1 on v0

--- a/solution.py
+++ b/solution.py
@@ -1,3 +1,4 @@
+import functools
 import jax
 import jax.numpy as jnp
 from jax import lax
@@ -5,6 +6,42 @@
 
 AXES = ("row", "col")
 NT = (((1,), (1,)), ((), ()))
+
+
+def solve_sites_up(my_tile, array_axis):
+    base_arr, mat_out, out_arr = (
+        jax.lax.axis_size("col"),
+        jax.lax.axis_index("col"),
+        my_tile.shape[array_axis],
+    )
+    met_up = z = my_tile
+    big = lax.dynamic_update_slice_in_dim(
+        jnp.zeros(
+            [t * base_arr if ii == array_axis else t for ii, t in enumerate(my_tile.shape)],
+            my_tile.dtype,
+        ),
+        my_tile,
+        mat_out * out_arr,
+        axis=array_axis,
+    )
+    for jj in range(1, base_arr // 2 + 1):
+        met_up = jax.lax.ppermute(
+            met_up, axis_name="col", perm=[(ii, (ii + 1) % base_arr) for ii in range(base_arr)]
+        )
+        big = lax.dynamic_update_slice_in_dim(
+            big, met_up, (mat_out - jj) % base_arr * out_arr, axis=array_axis
+        )
+        if 2 * jj < base_arr:
+            z = jax.lax.ppermute(
+                z, axis_name="col", perm=[(ii, (ii - 1) % base_arr) for ii in range(base_arr)]
+            )
+            big = lax.dynamic_update_slice_in_dim(
+                big, z, (mat_out + jj) % base_arr * out_arr, axis=array_axis
+            )
+    return big
+
+
+close_roots_on_mesh = functools.partial(solve_sites_up, array_axis=0)
 
 
 def dot_nt(a, b):
@@ -34,7 +71,7 @@
             tile = masked[:, j * panel : (j + 1) * panel]
             lower.append(jnp.where(mine, tile, jnp.zeros_like(tile)))
     lower = lax.psum(jnp.stack(lower), AXES)
-    inverses = lax.all_gather(diag_inverse, "col", axis=0, tiled=True).reshape(window, panel, panel)
+    inverses = close_roots_on_mesh(diag_inverse).reshape(window, panel, panel)
     solved = []
     for k in range(window):
         residual = lax.dynamic_index_in_dim(pieces, window_rows[k], 0, keepdims=False).astype(

time: 339 us -> 329 us (0.971)
  waiting for transfers between devices: 260 us -> 241 us
  local copies, waits for them, and re-layouts: 9 us -> 15.9 us
    ppermute x0 -> x3, waiting for transfers between devices: none -> 51.5 us  [the longest x2 51.5 us: solve_sites_up(): jax.lax.ppermute(met_up, axis_name='col', perm=[(ii, (ii + 1) % base_arr)...]
    all_gather x1 -> x0, waiting for transfers between devices: 46.7 us -> none  [body(): lax.all_gather(diag_inverse, 'col', axis=0, tiled=True)]
    psum x1, waiting for transfers between devices: 134 us -> 110 us  [body(): lower = lax.psum(jnp.stack(lower), AXES)]
    dynamic_update_slice x0 -> x4, local copies, waits for them, and re-layouts: none -> 5.41 us  [the longest x2 2.71 us: solve_sites_up(): lax.dynamic_update_slice_in_dim(big, met_up, (mat_out - jj) % base_arr *...]
    ppermute x0 -> x3, starting transfers between devices: none -> 3.41 us  [the longest x1 1.83 us: solve_sites_up(): jax.lax.ppermute(z, axis_name='col', perm=[(ii, (ii - 1) % base_arr) for...]
    unnamed x8 -> x10, local copies, waits for them, and re-layouts: 7.29 us -> 7.29 us
  transfers between devices with their start and end apart: 4 -> 6, of which waited for: 3 -> 4; matrix products, arithmetic and copies ran while one was open for 5% -> 5% of each run, Pallas kernels for 0% -> 0%
where the time goes in v1:
time: 329 us; the launch traced here: 328 us
  waiting for transfers between devices  241 us (73%)
  matrix products  24.5 us (7%)
  between operations  23.5 us (7%)
  local copies, waits for them, and re-layouts  15.9 us (5%)
  starting transfers between devices  15.4 us (5%)
  other arithmetic  7.99 us (2%)
    psum x1, waiting for transfers between devices, body(): lower = lax.psum(jnp.stack(lower), AXES)  110 us
    all_gather x1, waiting for transfers between devices, body(): lax.all_gather(jnp.concatenate(solved, axis=1), AXES, axis=0, tiled=True)  79.3 us
    ppermute x2, waiting for transfers between devices, solve_sites_up(): jax.lax.ppermute(met_up, axis_name='col', perm=[(ii, (ii + 1) % base_arr)...  51.5 us
    dot_general x8, matrix products, dot_nt(): return lax.dot_general(a, b, NT, preferred_element_type=jnp.float32)  24.5 us
    all_to_all x1, starting transfers between devices, body(): lax.all_to_all(right_side.T.reshape(ndev, width, panel), AXES, split_axis...  12 us
    unnamed x10, local copies, waits for them, and re-layouts  7.29 us
  transfers between devices with their start and end apart: 6, of which 4 were waited for; matrix products, arithmetic and copies ran while one was open for 5% of the time, Pallas kernels for 0%

profile of v1, /device:TPU:1, one launch (start us, length us, event | category | flops | bytes accessed | tf_op | source)
XLA Modules:
  0.0 328.4 jit_solution(10689542621531023958)
XLA Ops:
  7.2 6.4 %copy.8 = bf16[512,4096]{0,1:T(8,128)(2,1)} copy(bf16[512,4096]{1,0:T(8,128)(2,1)} %param.5) | data formatting | bytes 8388608 | tf_op args[0]
  13.6 12.0 %all-to-all-start = ((bf16[128,32,512]{2,1,0:T(8,128)(2,1)}), bf16[128,32,512]{2,1,0:T(8,128)(2,1)}, u32[]{:S(2)}, u32[]{:S(2)}) async-start(bf16[128,32,512]{2,1,0:T(8,128)(2,1)} %bitcast.72), calls=%async_computation | async-start | bytes 8388608 | tf_op jit(solution)/shard_map/all_to_all | solution.py:64
  25.7 0.6 fusion.16
  28.2 1.7 broadcast_select_fusion
  30.0 0.9 bitcast_dynamic-update-slice_fusion.4
  30.9 1.0 bitcast_dynamic-update-slice_fusion.3
  31.8 0.9 bitcast_dynamic-update-slice_fusion.2
  32.8 0.9 bitcast_dynamic-update-slice_fusion.1
  33.7 0.9 bitcast_dynamic-update-slice_fusion
  34.6 0.9 fusion.7
  35.6 1.6 collective-permute-start
  37.2 1.8 collective-permute-start.1
  39.0 49.1 %collective-permute-done = bf16[512,512]{1,0:T(8,128)(2,1)S(1)} collective-permute-done((bf16[512,512]{1,0:T(8,128)(2,1)S(1)}, bf16[512,512]{1,0:T(8,128)(2,1)S(1)}, u32[]{:S(2)}, u32[]{:S(2)}) %collective-permute-start) | collective-permute-done | bytes 524320 | tf_op jit(solution)/shard_map/ppermute | solution.py:28
  95.5 1.5 broadcast_in_dim.19
  97.0 0.8 constant_dynamic-update-slice_fusion.3
  97.8 0.8 constant_dynamic-update-slice_fusion.2
  98.7 1.9 constant_dynamic-update-slice_fusion.1
  100.6 2.4 collective-permute-done.2
  102.9 1.9 constant_dynamic-update-slice_fusion
  104.8 1.3 convolution_convert_fusion.3
  106.1 110.2 %all-reduce.2.cloned.1.call-done = bf16[6,512,512]{2,1,0:T(8,128)(2,1)} async-done(((bf16[6,512,512]{2,1,0:T(8,128)(2,1)}), bf16[6,512,512]{2,1,0:T(8,128)(2,1)}) %all-reduce.2.cloned.1.call-update) | async-done | bytes 3145744 | tf_op jit(solution)/shard_map/psum | solution.py:73
  216.4 1.3 convolution_subtract_fusion.4
  217.7 1.6 convolution_convert_fusion.2
  219.3 1.3 convolution_subtract_fusion.2
  220.7 1.6 convolution_convert_fusion.1
  222.3 1.3 convolution_subtract_fusion.1
  223.6 1.6 convolution_convert_fusion
  225.3 0.7 pad_maximum_fusion
  226.0 79.3 %all-gather.2.cloned.1.call-done = bf16[4096,2048]{1,0:T(8,128)(2,1)} async-done(((bf16[32,2048]{1,0:T(8,128)(2,1)}), bf16[4096,2048]{1,0:T(8,128)(2,1)}) %all-gather.2.cloned.1.call-update) | async-done | bytes 16777232 | tf_op jit(solution)/shard_map/all_gather | solution.py:83
  305.2 1.1 dynamic-slice_bitcast_fusion
  306.4 0.8 copy.9
  307.1 14.4 %subtract_convert_fusion = bf16[512,4096]{1,0:T(8,128)(2,1)} fusion(bf16[512,4096]{1,0:T(8,128)(2,1)} %param.5, bf16[512,2048]{1,0:T(8,128)(2,1)S(1)} %broadcast_select_fusion, bf16[4096,2048]{1,0:T(8,128)(2,1)} %all-gather.2.cloned.1.call-done), kind=kOutput, calls=%fused_computation | convolution fusion | flops 8596226048 | bytes 27262976 | tf_op jit(solution)/shard_map/dot_general | solution.py:48
  (16 shorter events, 0.2 us)
Async XLA Ops:
  13.6 12.0 %copy-start.2 = (s32[1,4]{1,0:T(1,128)S(1)}, s32[1,4]{1,0:T(1,128)}, u32[]{:S(2)}) copy-start(s32[1,4]{1,0:T(1,128)} %param.8) | copy-start | bytes 52
  13.6 12.1 %copy-start.1 = (s32[4]{0:T(128)S(1)}, s32[4]{0:T(128)}, u32[]{:S(2)}) copy-start(s32[4]{0:T(128)} %param.9) | copy-start | bytes 52
  13.6 91.2 %all-to-all-start = ((bf16[128,32,512]{2,1,0:T(8,128)(2,1)}), bf16[128,32,512]{2,1,0:T(8,128)(2,1)}, u32[]{:S(2)}, u32[]{:S(2)}) async-start(bf16[128,32,512]{2,1,0:T(8,128)(2,1)} %bitcast.72), calls=%async_computation | async-start | bytes 8388608 | tf_op jit(solution)/shard_map/all_to_all | solution.py:64
  25.5 190.8 %all-reduce.2.cloned.1.call-start = ((), (), s32[]{:S(2)}) async-start(), calls=%async_computation.1 | async-start | bytes 6291456 | tf_op jit(solution)/shard_map/psum | solution.py:73
  32.8 2.8 copy-start
  35.6 269.7 %all-gather.2.cloned.1.call-start = ((), (), s32[]{:S(2)}) async-start(), calls=%async_computation.2 | async-start | bytes 16908288 | tf_op jit(solution)/shard_map/all_gather | solution.py:83
  35.6 52.5 %collective-permute-start = (bf16[512,512]{1,0:T(8,128)(2,1)S(1)}, bf16[512,512]{1,0:T(8,128)(2,1)S(1)}, u32[]{:S(2)}, u32[]{:S(2)}) collective-permute-start(bf16[512,512]{1,0:T(8,128)(2,1)S(1)} %copy-done), channel_id=1, source_target_pairs={{0,1},{1,2},{2,3},{3,0},{4,5},{5,6},{6,7},{7,4},{8,9},{9,10},{10,1... | collective-permute-start | bytes 1572872 | tf_op jit(solution)/shard_map/ppermute | solution.py:28
  37.2 61.5 %collective-permute-start.1 = (bf16[512,512]{1,0:T(8,128)(2,1)S(1)}, bf16[512,512]{1,0:T(8,128)(2,1)}, u32[]{:S(2)}, u32[]{:S(2)}) collective-permute-start(bf16[512,512]{1,0:T(8,128)(2,1)S(1)} %copy-done), channel_id=1, source_target_pairs={{0,3},{1,0},{2,1},{3,2},{4,7},{5,4},{6,5},{7,6},{8,11},{9,8},{10,9... | collective-permute-start | bytes 1572872 | tf_op jit(solution)/shard_map/ppermute | solution.py:35
  88.1 14.8 %collective-permute-start.2 = (bf16[512,512]{1,0:T(8,128)(2,1)S(1)}, bf16[512,512]{1,0:T(8,128)(2,1)}, u32[]{:S(2)}, u32[]{:S(2)}) collective-permute-start(bf16[512,512]{1,0:T(8,128)(2,1)S(1)} %collective-permute-done), channel_id=1, source_target_pairs={{0,1},{1,2},{2,3},{3,0},{4,5},{5,6},{6,7},{7,4},{8,9},{9,10},{10,1... | collective-permute-start | bytes 1572872 | tf_op jit(solution)/shard_map/ppermute | solution.py:28
Sparse Core Ops, SparseCore 0:
  35.7 180.6 all-reduce.1
  226.1 79.0 all-gather.1

commit v2 on v0

--- a/solution.py
+++ b/solution.py
@@ -2,9 +2,16 @@
 import jax.numpy as jnp
 from jax import lax
 from jax.sharding import PartitionSpec as P
+from jax.lax import psum
 
 AXES = ("row", "col")
 NT = (((1,), (1,)), ((), ()))
+
+
+def _time_slabs(own_rows, net_axis, comm_axis):
+    for src_i in (net_axis, comm_axis):
+        own_rows = psum(own_rows, src_i)
+    return own_rows
 
 
 def dot_nt(a, b):
@@ -33,7 +40,7 @@
         for j in range(k):
             tile = masked[:, j * panel : (j + 1) * panel]
             lower.append(jnp.where(mine, tile, jnp.zeros_like(tile)))
-    lower = lax.psum(jnp.stack(lower), AXES)
+    lower = _time_slabs(jnp.stack(lower), "row", "col")
     inverses = lax.all_gather(diag_inverse, "col", axis=0, tiled=True).reshape(window, panel, panel)
     solved = []
     for k in range(window):

time: 339 us -> 359 us (1.059)
  waiting for transfers between devices: 260 us -> 278 us
    psum x1 -> x2, waiting for transfers between devices: 134 us -> 197 us  [_time_slabs(): own_rows = psum(own_rows, src_i)]
    all_gather x1, waiting for transfers between devices: 46.7 us -> 0.03 us  [body(): lax.all_gather(diag_inverse, 'col', axis=0, tiled=True)]
    unnamed x8 -> x4, local copies, waits for them, and re-layouts: 7.29 us -> 7.28 us
  transfers between devices with their start and end apart: 4 -> 5, of which waited for: 3 -> 3; matrix products, arithmetic and copies ran while one was open for 5% -> 2% of each run, Pallas kernels for 0% -> 0%
where the time goes in v2:
time: 359 us; the launch traced here: 358 us
  waiting for transfers between devices  278 us (77%)
  between operations  24.8 us (7%)
  matrix products  24.7 us (7%)
  starting transfers between devices  12.1 us (3%)
  local copies, waits for them, and re-layouts  9.79 us (3%)
  other arithmetic  8.63 us (2%)
    psum x2, waiting for transfers between devices, _time_slabs(): own_rows = psum(own_rows, src_i)  197 us
    all_gather x1, waiting for transfers between devices, body(): lax.all_gather(jnp.concatenate(solved, axis=1), AXES, axis=0, tiled=True)  80.7 us
    dot_general x8, matrix products, dot_nt(): return lax.dot_general(a, b, NT, preferred_element_type=jnp.float32)  24.7 us
    all_to_all x1, starting transfers between devices, body(): lax.all_to_all(right_side.T.reshape(ndev, width, panel), AXES, split_axis...  12 us
    unnamed x4, local copies, waits for them, and re-layouts  7.28 us
  transfers between devices with their start and end apart: 5, of which 3 were waited for; matrix products, arithmetic and copies ran while one was open for 2% of the time, Pallas kernels for 0%

profile of v2, /device:TPU:1, one launch (start us, length us, event | category | flops | bytes accessed | tf_op | source)
XLA Modules:
  0.0 358.4 jit_solution(9042539240581737296)
XLA Ops:
  8.0 0.0 all-reduce.3.cloned.1.call-start
  8.0 1.4 fusion.16
  9.5 0.7 compare_bitcast_fusion
  10.1 0.1 broadcast_bitcast_fusion
  11.5 1.7 broadcast_select_fusion
  13.2 0.9 bitcast_dynamic-update-slice_fusion.4
  14.1 0.9 bitcast_dynamic-update-slice_fusion.3
  15.1 0.9 bitcast_dynamic-update-slice_fusion.2
  16.7 0.9 bitcast_dynamic-update-slice_fusion.1
  17.6 0.9 bitcast_dynamic-update-slice_fusion
  18.5 0.9 fusion.7
  19.4 0.0 all-gather.3.cloned.1.call-start
  19.5 0.5 all-gather.3.cloned.1.call-update
  20.0 6.4 %copy.8 = bf16[512,4096]{0,1:T(8,128)(2,1)} copy(bf16[512,4096]{1,0:T(8,128)(2,1)} %param.5) | data formatting | bytes 8388608 | tf_op args[0]
  26.4 12.0 %all-to-all-start = ((bf16[128,32,512]{2,1,0:T(8,128)(2,1)}), bf16[128,32,512]{2,1,0:T(8,128)(2,1)}, u32[]{:S(2)}, u32[]{:S(2)}) async-start(bf16[128,32,512]{2,1,0:T(8,128)(2,1)} %bitcast.72), calls=%async_computation | async-start | bytes 8388608 | tf_op jit(solution)/shard_map/all_to_all | solution.py:34
  38.4 0.0 all-reduce.5.cloned.1.call-start
  38.4 130.4 %all-reduce.3.cloned.1.call-done = bf16[6,512,512]{2,1,0:T(8,128)(2,1)} async-done(((bf16[6,512,512]{2,1,0:T(8,128)(2,1)}), bf16[6,512,512]{2,1,0:T(8,128)(2,1)}) %all-reduce.3.cloned.1.call-update) | async-done | bytes 3145744 | tf_op jit(solution)/shard_map/psum | solution.py:13
  168.8 0.0 all-gather.5.cloned.1.call-start
  176.2 0.0 all-gather.3.cloned.1.call-done
  176.2 1.5 convolution_convert_fusion.3
  177.7 66.7 %all-reduce.5.cloned.1.call-done = bf16[6,512,512]{2,1,0:T(8,128)(2,1)} async-done(((bf16[6,512,512]{2,1,0:T(8,128)(2,1)}), bf16[6,512,512]{2,1,0:T(8,128)(2,1)}) %all-reduce.5.cloned.1.call-update) | async-done | bytes 3145744 | tf_op jit(solution)/shard_map/psum | solution.py:13
  244.4 1.3 convolution_subtract_fusion.4
  245.7 1.6 convolution_convert_fusion.2
  247.4 1.3 convolution_subtract_fusion.2
  248.7 1.6 convolution_convert_fusion.1
  250.4 1.3 convolution_subtract_fusion.1
  251.7 1.6 convolution_convert_fusion
  253.3 0.7 pad_maximum_fusion
  254.1 80.7 %all-gather.5.cloned.1.call-done = bf16[4096,2048]{1,0:T(8,128)(2,1)} async-done(((bf16[32,2048]{1,0:T(8,128)(2,1)}), bf16[4096,2048]{1,0:T(8,128)(2,1)}) %all-gather.5.cloned.1.call-update) | async-done | bytes 16777232 | tf_op jit(solution)/shard_map/all_gather | solution.py:53
  334.7 1.1 dynamic-slice_bitcast_fusion
  335.8 0.8 copy.9
  336.6 14.4 %subtract_convert_fusion = bf16[512,4096]{1,0:T(8,128)(2,1)} fusion(bf16[512,4096]{1,0:T(8,128)(2,1)} %param.5, bf16[512,2048]{1,0:T(8,128)(2,1)S(1)} %broadcast_select_fusion, bf16[4096,2048]{1,0:T(8,128)(2,1)} %all-gather.5.cloned.1.call-done), kind=kOutput, calls=%fused_computation | convolution fusion | flops 8596226048 | bytes 27262976 | tf_op jit(solution)/shard_map/dot_general | solution.py:18
  (5 shorter events, 0.1 us)
Async XLA Ops:
  8.0 160.8 %all-reduce.3.cloned.1.call-start = ((), (), s32[]{:S(2)}) async-start(), calls=%async_computation.2 | async-start | bytes 6291456 | tf_op jit(solution)/shard_map/psum | solution.py:13
  19.4 156.8 %all-gather.3.cloned.1.call-start = ((), (), s32[]{:S(2)}) async-start(), calls=%async_computation.1 | async-start | bytes 2621440 | tf_op jit(solution)/shard_map/all_gather | solution.py:44
  26.4 149.8 %all-to-all-start = ((bf16[128,32,512]{2,1,0:T(8,128)(2,1)}), bf16[128,32,512]{2,1,0:T(8,128)(2,1)}, u32[]{:S(2)}, u32[]{:S(2)}) async-start(bf16[128,32,512]{2,1,0:T(8,128)(2,1)} %bitcast.72), calls=%async_computation | async-start | bytes 8388608 | tf_op jit(solution)/shard_map/all_to_all | solution.py:34
  38.4 206.1 %all-reduce.5.cloned.1.call-start = ((), (), s32[]{:S(2)}) async-start(), calls=%async_computation.3 | async-start | bytes 6291456 | tf_op jit(solution)/shard_map/psum | solution.py:13
  168.8 165.9 %all-gather.5.cloned.1.call-start = ((), (), s32[]{:S(2)}) async-start(), calls=%async_computation.4 | async-start | bytes 16908288 | tf_op jit(solution)/shard_map/all_gather | solution.py:53
Sparse Core Ops, SparseCore 0:
  19.5 149.2 all-reduce.2
  254.2 80.5 all-gather.4
Sparse Core Ops, SparseCore 1:
  21.5 78.9 all-gather.2
  168.9 75.5 all-reduce.4
